TPU v7x, 512 devices: a whole 4x4x16 slice. The times are simulated.
512 devices in a mesh: group: 16 (over z), shard: 32 (over y, x, core).
Axes of the slice: x: 4, y: 4, z: 16, core: 2. Of those that a mesh axis runs over, the one named last changes fastest.
Arguments:
- hot_row: int32 [4096, 39], P(('group', 'shard')), may hold values from 0 to 2047
- cold_row: int32 [4096, 39], P(('group', 'shard')), may hold values from 0 to 4095
- cold_owner: int32 [4096, 39], P(('group', 'shard')), may hold values from 0 to 31, as said below
- is_cold: int32 [4096, 39], P(('group', 'shard')), may hold values from 0 to 1
- grad_logit: float32 [4096], P(('group', 'shard')), may hold values from -12 to 12
- hot_table: bfloat16 [2048, 128], replicated, may hold values from -6 to 6
- cold_table: bfloat16 [131072, 128], P('shard'), may hold values from -6 to 6
- first_weight: bfloat16 [100, 1521], replicated, may hold values from -0.15625 to 0.15625
- second_weight: bfloat16 [100, 3900], replicated, may hold values from -0.09375 to 0.09375
- third_weight: bfloat16 [100, 3900], replicated, may hold values from -0.09375 to 0.09375
- out_weight: float32 [3, 100], replicated, may hold values from -0.375 to 0.375
Outputs:
- hot_grad: bfloat16 [2048, 128], replicated
- cold_grad: bfloat16 [131072, 128], P('shard')
- logits: float32 [4096], P(('group', 'shard'))
Inputs may be any that keep to these rules, and one draw needn't show every extreme that they name: `cold_owner`: among the 312 lookups of one device, at most 9 with is_cold 1 name the same owner; for each index of group, one owner receives exactly 9 such lookups from every device of that group index.
All inputs are finite; a program needn't handle non-finite values.
Results may differ from a plain program's by a relative error of at most 0.014.
Values may be sent and summed in bfloat16 or wider, within the bound.
No kernel may reach another device: no remote copies, remote signals or barrier semaphores. Data moves between devices by JAX's collectives and lax.ppermute only.
A program may use at most 64 MiB of HBM per device.

v0:
```python
import jax
import jax.numpy as jnp
from jax import lax
from jax.sharding import PartitionSpec as P


def sample_pass(embedded, grad_logit, layer_weights, out_weight):
    batch_rows, fields, breadth = embedded.shape
    base_wide = embedded.astype(jnp.float32)
    previous = embedded
    layer_inputs = []
    logit_sum = jnp.zeros((batch_rows,), jnp.float32)
    for section_index in range(len(layer_weights)):
        weight = layer_weights[section_index]
        below_maps = previous.shape[1]
        outer_rows = (
            previous.astype(jnp.float32)[:, :, None, :] * base_wide[:, None, :, :]
        ).astype(jnp.bfloat16)
        outer_rows = outer_rows.reshape(batch_rows, below_maps * fields, breadth)
        current = jnp.einsum(
            "hk,bke->bhe", weight, outer_rows, preferred_element_type=jnp.float32
        ).astype(jnp.bfloat16)
        pooled = jnp.sum(current.astype(jnp.float32), axis=2)
        logit_sum = logit_sum + jnp.sum(pooled * out_weight[section_index][None, :], axis=1)
        layer_inputs.append(previous)
        previous = current
    grad_embedded = jnp.zeros((batch_rows, fields, breadth), jnp.float32)
    carried = jnp.zeros((batch_rows, out_weight.shape[1], breadth), jnp.float32)
    for section_index in reversed(range(len(layer_weights))):
        weight = layer_weights[section_index]
        lower_state = layer_inputs[section_index]
        below_maps = lower_state.shape[1]
        grad_state = carried + grad_logit[:, None, None] * out_weight[section_index][None, :, None]
        grad_low = grad_state.astype(jnp.bfloat16)
        grad_outer = jnp.einsum("hk,bhe->bke", weight, grad_low, preferred_element_type=jnp.float32)
        grad_outer = grad_outer.reshape(batch_rows, below_maps, fields, breadth)
        grad_embedded = grad_embedded + jnp.sum(
            grad_outer * lower_state.astype(jnp.float32)[:, :, None, :], axis=1
        )
        carried = jnp.sum(grad_outer * base_wide[:, None, :, :], axis=2)
    grad_embedded = grad_embedded + carried
    return (logit_sum, grad_embedded)


def local(
    hot_row,
    cold_row,
    cold_owner,
    is_cold,
    grad_logit,
    hot_table,
    cold_table,
    first_weight,
    second_weight,
    third_weight,
    out_weight,
):
    samples, fields = hot_row.shape
    breadth = hot_table.shape[1]
    owners = lax.axis_size("shard")
    lookups = samples * fields
    capacity = lookups // owners
    owner_flat = cold_owner.reshape(lookups)
    cold_flag = is_cold.reshape(lookups) == 1
    wanted = jnp.logical_and(
        owner_flat[:, None] == jnp.arange(owners, dtype=jnp.int32)[None, :], cold_flag[:, None]
    ).astype(jnp.int32)
    earlier = jnp.cumsum(wanted, axis=0) - wanted
    position = jnp.sum(earlier * wanted, axis=1)
    target = jnp.where(cold_flag, owner_flat * capacity + position, owners * capacity)
    asked_rows = jnp.where(cold_flag, cold_row.reshape(lookups), -1)
    request = jnp.full((owners * capacity + 1,), -1, jnp.int32).at[target].set(asked_rows)
    request = request[: owners * capacity].reshape(owners, capacity)
    requested = lax.all_to_all(request, "shard", split_axis=0, concat_axis=0, tiled=True)
    present = requested >= 0
    table_rows = jnp.take(cold_table, jnp.maximum(requested, 0), axis=0)
    table_rows = jnp.where(present[:, :, None], table_rows, jnp.zeros_like(table_rows))
    returned = lax.all_to_all(table_rows, "shard", split_axis=0, concat_axis=0, tiled=True)
    fetched_flat = jnp.concatenate(
        [returned.reshape(owners * capacity, breadth), jnp.zeros((1, breadth), jnp.bfloat16)],
        axis=0,
    )
    cold_values = jnp.take(fetched_flat, target, axis=0)
    hot_values = jnp.take(hot_table, hot_row.reshape(lookups), axis=0)
    embedded = jnp.where(cold_flag[:, None], cold_values, hot_values).reshape(
        samples, fields, breadth
    )
    layer_weights = (first_weight, second_weight, third_weight)

    def one_sample(sample_pair):
        logit_one, grad_one = sample_pass(
            sample_pair[0][None], sample_pair[1][None], layer_weights, out_weight
        )
        return (logit_one[0], grad_one[0])

    logits, gradients = lax.map(one_sample, (embedded, grad_logit))
    gradients = gradients.reshape(lookups, breadth)
    cold_terms = jnp.where(cold_flag[:, None], gradients, 0.0)
    hot_terms = jnp.where(cold_flag[:, None], 0.0, gradients)
    outgoing = jnp.zeros((owners * capacity + 1, breadth), jnp.float32).at[target].add(cold_terms)
    outgoing = outgoing[: owners * capacity].reshape(owners, capacity, breadth)
    incoming = lax.all_to_all(
        outgoing.astype(jnp.bfloat16), "shard", split_axis=0, concat_axis=0, tiled=True
    ).astype(outgoing.dtype)
    shard_rows = cold_table.shape[0]
    safe_ids = jnp.maximum(requested, 0)
    cold_local = jax.ops.segment_sum(
        incoming.reshape(-1, breadth), safe_ids.reshape(-1), num_segments=shard_rows
    )
    cold_total = lax.psum(cold_local.astype(jnp.bfloat16), "group")
    hot_local = jax.ops.segment_sum(
        hot_terms, hot_row.reshape(lookups), num_segments=hot_table.shape[0]
    )
    hot_grad = lax.psum(hot_local, ("group", "shard")).astype(jnp.bfloat16)
    return (hot_grad, cold_total, logits)


def solution(mesh):
    return jax.shard_map(
        local,
        mesh=mesh,
        in_specs=(
            P(("group", "shard"), None),
            P(("group", "shard"), None),
            P(("group", "shard"), None),
            P(("group", "shard"), None),
            P(("group", "shard")),
            P(),
            P("shard", None),
            P(),
            P(),
            P(),
            P(),
        ),
        out_specs=(P(), P("shard", None), P(("group", "shard"))),
        check_vma=False,
    )
```

profile of v0, /device:TPU:2, one launch (start us, length us, event | category | flops | bytes accessed | tf_op | source)
XLA Modules:
  0.0 380.4 jit_solution(5741558667474088209)
XLA Ops:
  11.8 2.9 scatter_custom_fusion
  15.4 9.4 %all-to-all-start = ((s32[32,1,9]{2,1,0:T(1,128)}), s32[32,1,9]{2,1,0:T(1,128)S(1)}, u32[]{:S(2)}, u32[]{:S(2)}) async-start(s32[32,1,9]{2,1,0:T(1,128)} %bitcast.28), calls=%async_computation | async-start | bytes 32768 | tf_op jit(solution)/shard_map/all_to_all | solution.py:74
  26.5 2.3 gather_fusion.2
  28.8 2.2 all-to-all-done
  31.3 1.4 gather_fusion
  33.8 5.3 %all-to-all-start.1 = ((bf16[32,9,128]{2,1,0:T(8,128)(2,1)}), bf16[32,9,128]{2,1,0:T(8,128)(2,1)S(1)}, u32[]{:S(2)}, u32[]{:S(2)}) async-start(bf16[32,9,128]{2,1,0:T(8,128)(2,1)} %select_select_fusion), calls=%async_computation.1 | async-start | bytes 262144 | tf_op jit(solution)/shard_map/all_to_all | solution.py:78
  39.2 6.5 %all-to-all-done.1 = bf16[32,9,128]{2,1,0:T(8,128)(2,1)S(1)} async-done(((bf16[32,9,128]{2,1,0:T(8,128)(2,1)}), bf16[32,9,128]{2,1,0:T(8,128)(2,1)S(1)}, u32[]{:S(2)}, u32[]{:S(2)}) %all-to-all-start.1) | async-done | bytes 73760 | tf_op jit(solution)/shard_map/all_to_all | solution.py:78
  45.8 1.4 gather_fusion.1
  48.1 165.5 %while.12 = (s32[]{:T(128)}, f32[8]{0:T(128)}, f32[8,39,128]{2,1,0:T(8,128)}, bf16[8,39,128]{2,1,0:T(8,128)(2,1)}, bf16[100,1521]{1,0:T(8,128)(2,1)S(1)}, /*inde...) while((s32[]{:T(128)}, f32[8]{0:T(128)}, ...), condition=%wide.region_17.18_spmd, body=%wide.region_4.17_spmd.sunk | while | flops 484535232 | bytes 39531044 | solution.py:96
  49.8 1.6 fusion.65
  52.0 1.7 fusion.66
  56.3 1.8 convolution_bitcast_fusion.6
  58.2 1.6 reshape.545
  60.9 1.8 convolution_bitcast_fusion.7
  62.8 1.6 reshape.546
  70.5 1.6 fusion.65
  72.7 1.7 fusion.66
  77.0 1.8 convolution_bitcast_fusion.6
  78.9 1.6 reshape.545
  81.6 1.8 convolution_bitcast_fusion.7
  83.5 1.6 reshape.546
  91.2 1.6 fusion.65
  93.3 1.7 fusion.66
  97.7 1.8 convolution_bitcast_fusion.6
  99.6 1.6 reshape.545
  102.3 1.8 convolution_bitcast_fusion.7
  104.1 1.6 reshape.546
  111.9 1.6 fusion.65
  114.0 1.7 fusion.66
  118.4 1.8 convolution_bitcast_fusion.6
  120.2 1.6 reshape.545
  123.0 1.8 convolution_bitcast_fusion.7
  124.8 1.6 reshape.546
  132.6 1.6 fusion.65
  134.7 1.7 fusion.66
  139.1 1.8 convolution_bitcast_fusion.6
  140.9 1.6 reshape.545
  143.7 1.8 convolution_bitcast_fusion.7
  145.5 1.6 reshape.546
  153.2 1.6 fusion.65
  155.4 1.7 fusion.66
  159.7 1.8 convolution_bitcast_fusion.6
  161.6 1.6 reshape.545
  164.3 1.8 convolution_bitcast_fusion.7
  166.2 1.6 reshape.546
  173.9 1.6 fusion.65
  176.1 1.7 fusion.66
  180.4 1.8 convolution_bitcast_fusion.6
  182.3 1.6 reshape.545
  185.0 1.8 convolution_bitcast_fusion.7
  186.9 1.6 reshape.546
  194.6 1.6 fusion.65
  196.8 1.7 fusion.66
  201.1 1.8 convolution_bitcast_fusion.6
  203.0 1.6 reshape.545
  205.7 1.8 convolution_bitcast_fusion.7
  207.5 1.6 reshape.546
  214.5 2.0 scatter_custom_fusion.2
  216.6 11.5 %all_to_all.19 = bf16[32,9,128]{2,1,0:T(8,128)(2,1)S(1)} all-to-all(bf16[32,9,128]{2,1,0:T(8,128)(2,1)S(1)} %convert_element_type.112), channel_id=1, replica_groups=mesh['group'=16,'shard'=32] {'shard'}, dimensions={0} | all-to-all | bytes 147456 | tf_op jit(solution)/shard_map/all_to_all | solution.py:102
  228.2 2.5 scatter_custom_fusion.3
  231.9 2.0 scatter_custom_fusion.1
  233.9 110.9 %all-reduce.6 = bf16[2048,128]{1,0:T(8,128)(2,1)} all-reduce(f32[2048,128]{1,0:T(8,128)S(1)} %scatter_custom_fusion.1), channel_id=1, replica_groups=mesh['group'=16,'shard'=32] {'group','shard'}, use_global_device_ids=true, to_apply=%region_19.20 | all-reduce | flops 262144 | bytes 1572864 | tf_op jit(solution)/shard_map/psum | solution.py:114
  344.8 26.5 %all-reduce.5.cloned.1.call-done = bf16[4096,128]{1,0:T(8,128)(2,1)} async-done(((bf16[4096,128]{1,0:T(8,128)(2,1)}), bf16[4096,128]{1,0:T(8,128)(2,1)}) %all-reduce.5.cloned.1.call-update) | async-done | bytes 1048592 | tf_op jit(solution)/shard_map/psum | solution.py:110
  371.3 2.3 copy.47
  (280 shorter events, 80.0 us)
Async XLA Ops:
  7.2 24.2 %copy-start = (bf16[4096,128]{1,0:T(8,128)(2,1)S(1)}, bf16[4096,128]{1,0:T(8,128)(2,1)}, u32[]{:S(2)}) copy-start(bf16[4096,128]{1,0:T(8,128)(2,1)} %param.19) | copy-start | bytes 3145732
  8.0 23.3 %copy-start.7 = (pred[312]{0:T(512)(128)(4,1)}, pred[312]{0:T(512)(128)(4,1)S(1)}, u32[]{:S(2)}) copy-start(pred[312]{0:T(512)(128)(4,1)S(1)} %eq.48) | copy-start | bytes 940
  11.8 35.4 %copy-start.9 = (s32[312]{0:T(512)}, s32[312]{0:T(512)S(1)}, u32[]{:S(2)}) copy-start(s32[312]{0:T(512)S(1)} %fusion.26) | copy-start | bytes 3748
  15.4 15.6 %all-to-all-start = ((s32[32,1,9]{2,1,0:T(1,128)}), s32[32,1,9]{2,1,0:T(1,128)S(1)}, u32[]{:S(2)}, u32[]{:S(2)}) async-start(s32[32,1,9]{2,1,0:T(1,128)} %bitcast.28), calls=%async_computation | async-start | bytes 32768 | tf_op jit(solution)/shard_map/all_to_all | solution.py:74
  26.4 21.7 %copy-start.3 = (bf16[100,1521]{1,0:T(8,128)(2,1)S(1)}, bf16[100,1521]{1,0:T(8,128)(2,1)}, u32[]{:S(2)}) copy-start(bf16[100,1521]{1,0:T(8,128)(2,1)} %param.20) | copy-start | bytes 912604
  26.4 21.6 %copy-start.6 = (f32[3,100]{1,0:T(4,128)S(1)}, f32[3,100]{1,0:T(4,128)}, u32[]{:S(2)}) copy-start(f32[3,100]{1,0:T(4,128)} %param.23) | copy-start | bytes 3604
  31.3 7.8 %copy-start.10 = (s32[288]{0:T(512)}, s32[288]{0:T(512)S(1)}, u32[]{:S(2)}) copy-start(s32[288]{0:T(512)S(1)} %reshape.473) | copy-start | bytes 3460
  33.8 11.9 %all-to-all-start.1 = ((bf16[32,9,128]{2,1,0:T(8,128)(2,1)}), bf16[32,9,128]{2,1,0:T(8,128)(2,1)S(1)}, u32[]{:S(2)}, u32[]{:S(2)}) async-start(bf16[32,9,128]{2,1,0:T(8,128)(2,1)} %select_select_fusion), calls=%async_computation.1 | async-start | bytes 262144 | tf_op jit(solution)/shard_map/all_to_all | solution.py:78
  39.1 332.2 %all-reduce.5.cloned.1.call-start = ((), (), s32[]{:S(2)}) async-start(), calls=%async_computation.3 | async-start | bytes 2097152 | tf_op jit(solution)/shard_map/psum | solution.py:110
  52.0 4.4 %copy-start.2 = (bf16[100,3900]{1,0:T(8,128)(2,1)S(1)}, bf16[100,3900]{1,0:T(8,128)(2,1)}, u32[]{:S(2)}) copy-start(bf16[100,3900]{1,0:T(8,128)(2,1)} %get-tuple-element.208) | copy-start | bytes 2340004 | tf_op jit(solution)/shard_map/while
  59.8 1.1 copy-start.1
  65.0 0.7 copy-start.4
  65.0 3.1 copy-start.11
  68.3 0.5 copy-start.12
  72.7 4.4 %copy-start.2 = (bf16[100,3900]{1,0:T(8,128)(2,1)S(1)}, bf16[100,3900]{1,0:T(8,128)(2,1)}, u32[]{:S(2)}) copy-start(bf16[100,3900]{1,0:T(8,128)(2,1)} %get-tuple-element.208) | copy-start | bytes 2340004 | tf_op jit(solution)/shard_map/while
  80.5 1.1 copy-start.1
  85.7 0.7 copy-start.4
  85.7 3.1 copy-start.11
  88.9 0.5 copy-start.12
  93.3 4.4 %copy-start.2 = (bf16[100,3900]{1,0:T(8,128)(2,1)S(1)}, bf16[100,3900]{1,0:T(8,128)(2,1)}, u32[]{:S(2)}) copy-start(bf16[100,3900]{1,0:T(8,128)(2,1)} %get-tuple-element.208) | copy-start | bytes 2340004 | tf_op jit(solution)/shard_map/while
  101.1 1.1 copy-start.1
  106.3 0.7 copy-start.4
  106.4 3.1 copy-start.11
  109.6 0.5 copy-start.12
  114.0 4.4 %copy-start.2 = (bf16[100,3900]{1,0:T(8,128)(2,1)S(1)}, bf16[100,3900]{1,0:T(8,128)(2,1)}, u32[]{:S(2)}) copy-start(bf16[100,3900]{1,0:T(8,128)(2,1)} %get-tuple-element.208) | copy-start | bytes 2340004 | tf_op jit(solution)/shard_map/while
  121.8 1.1 copy-start.1
  127.0 0.7 copy-start.4
  127.0 3.1 copy-start.11
  130.3 0.5 copy-start.12
  134.7 4.4 %copy-start.2 = (bf16[100,3900]{1,0:T(8,128)(2,1)S(1)}, bf16[100,3900]{1,0:T(8,128)(2,1)}, u32[]{:S(2)}) copy-start(bf16[100,3900]{1,0:T(8,128)(2,1)} %get-tuple-element.208) | copy-start | bytes 2340004 | tf_op jit(solution)/shard_map/while
  142.5 1.1 copy-start.1
  147.7 0.7 copy-start.4
  147.7 3.1 copy-start.11
  151.0 0.5 copy-start.12
  155.4 4.4 %copy-start.2 = (bf16[100,3900]{1,0:T(8,128)(2,1)S(1)}, bf16[100,3900]{1,0:T(8,128)(2,1)}, u32[]{:S(2)}) copy-start(bf16[100,3900]{1,0:T(8,128)(2,1)} %get-tuple-element.208) | copy-start | bytes 2340004 | tf_op jit(solution)/shard_map/while
  163.2 1.1 copy-start.1
  168.4 0.7 copy-start.4
  168.4 3.1 copy-start.11
  171.7 0.5 copy-start.12
  176.1 4.4 %copy-start.2 = (bf16[100,3900]{1,0:T(8,128)(2,1)S(1)}, bf16[100,3900]{1,0:T(8,128)(2,1)}, u32[]{:S(2)}) copy-start(bf16[100,3900]{1,0:T(8,128)(2,1)} %get-tuple-element.208) | copy-start | bytes 2340004 | tf_op jit(solution)/shard_map/while
  183.9 1.1 copy-start.1
  189.1 0.7 copy-start.4
  189.1 3.1 copy-start.11
  192.4 0.5 copy-start.12
  196.7 4.4 %copy-start.2 = (bf16[100,3900]{1,0:T(8,128)(2,1)S(1)}, bf16[100,3900]{1,0:T(8,128)(2,1)}, u32[]{:S(2)}) copy-start(bf16[100,3900]{1,0:T(8,128)(2,1)} %get-tuple-element.208) | copy-start | bytes 2340004 | tf_op jit(solution)/shard_map/while
  204.6 1.1 copy-start.1
  209.8 0.7 copy-start.4
  209.8 3.1 copy-start.11
  213.0 0.5 copy-start.12
  230.7 1.1 copy-start.5
  230.7 1.2 copy-start.8
Sparse Core Ops, SparseCore 0:
  231.9 139.3 all-reduce.4
where the time goes:
time: 383 us; the launch traced here: 380 us
  blocking collectives  122 us (32%)
  local copies, waits for them, and re-layouts  63.4 us (17%)
  matrix products  62.2 us (16%)
  other arithmetic  52.6 us (14%)
  waiting for transfers between devices  35.3 us (9%)
  loops' own time  15.5 us (4%)
  starting transfers between devices  14.7 us (4%)
  between operations  14.3 us (4%)
    psum x1, blocking collectives, local(): hot_grad = lax.psum(hot_local, ('group', 'shard')).astype(jnp.bfloat16)  111 us
    dot_general x24, matrix products, sample_pass(): jnp.einsum('hk,bhe->bke', weight, grad_low, preferred_element_type=jnp.fl...  33 us
    dot_general x24, matrix products, sample_pass(): jnp.einsum('hk,bke->bhe', weight, outer_rows, preferred_element_type=jnp....  29.2 us
    psum x1, waiting for transfers between devices, local(): cold_total = lax.psum(cold_local.astype(jnp.bfloat16), 'group')  26.5 us
    reshape x24, local copies, waits for them, and re-layouts, sample_pass(): grad_outer = grad_outer.reshape(batch_rows, below_maps, fields, breadth)  25.9 us
    another operation x1, loops' own time, local(): logits, gradients = lax.map(one_sample, (embedded, grad_logit))  15.5 us
    reduce_sum x24, other arithmetic, sample_pass(): jnp.sum(grad_outer * lower_state.astype(jnp.float32)[:, :, None, :], axis=1)  15.3 us
    all_to_all x1, blocking collectives, local(): lax.all_to_all(outgoing.astype(jnp.bfloat16), 'shard', split_axis=0, conc...  11.5 us
  transfers between devices with their start and end apart: 3, of which 3 were waited for; matrix products, arithmetic and copies ran while one was open for 2% of the time, Pallas kernels for 0%

commit v1 on v0

--- a/solution.py
+++ b/solution.py
@@ -111,7 +111,7 @@
     hot_local = jax.ops.segment_sum(
         hot_terms, hot_row.reshape(lookups), num_segments=hot_table.shape[0]
     )
-    hot_grad = lax.psum(hot_local, ("group", "shard")).astype(jnp.bfloat16)
+    hot_grad = lax.psum(lax.psum(hot_local, "shard"), "group").astype(jnp.bfloat16)
     return (hot_grad, cold_total, logits)
 
 

time: 383 us -> 510 us (1.33)
  waiting for transfers between devices: 35.3 us -> 194 us
  blocking collectives: 122 us -> 86.4 us
    psum x0 -> x1, waiting for transfers between devices: none -> 118 us  [local(): lax.psum(hot_local, 'shard')]
    psum x1, waiting for transfers between devices: 26.5 us -> 68.1 us  [local(): cold_total = lax.psum(cold_local.astype(jnp.bfloat16), 'group')]
    psum x1, blocking collectives: 111 us -> 75.1 us  [local(): lax.psum(lax.psum(hot_local, 'shard'), 'group').astype(jnp.bfloat16)]
  transfers between devices with their start and end apart: 3 -> 4, of which waited for: 3 -> 4; matrix products, arithmetic and copies ran while one was open for 2% -> 2% of each run, Pallas kernels for 0% -> 0%
where the time goes in v1:
time: 510 us; the launch traced here: 507 us
  waiting for transfers between devices  194 us (38%)
  blocking collectives  86.4 us (17%)
  local copies, waits for them, and re-layouts  64.6 us (13%)
  matrix products  62.3 us (12%)
  other arithmetic  53.5 us (10%)
  starting transfers between devices  16.1 us (3%)
  loops' own time  15.9 us (3%)
  between operations  14.3 us (3%)
    psum x1, waiting for transfers between devices, local(): lax.psum(hot_local, 'shard')  118 us
    psum x1, blocking collectives, local(): lax.psum(lax.psum(hot_local, 'shard'), 'group').astype(jnp.bfloat16)  75.1 us
    psum x1, waiting for transfers between devices, local(): cold_total = lax.psum(cold_local.astype(jnp.bfloat16), 'group')  68.1 us
    dot_general x24, matrix products, sample_pass(): jnp.einsum('hk,bhe->bke', weight, grad_low, preferred_element_type=jnp.fl...  33 us
    dot_general x24, matrix products, sample_pass(): jnp.einsum('hk,bke->bhe', weight, outer_rows, preferred_element_type=jnp....  29.3 us
    reshape x24, local copies, waits for them, and re-layouts, sample_pass(): grad_outer = grad_outer.reshape(batch_rows, below_maps, fields, breadth)  25.9 us
    another operation x1, loops' own time, local(): logits, gradients = lax.map(one_sample, (embedded, grad_logit))  15.9 us
    reduce_sum x24, other arithmetic, sample_pass(): jnp.sum(grad_outer * lower_state.astype(jnp.float32)[:, :, None, :], axis=1)  15.3 us
  transfers between devices with their start and end apart: 4, of which 4 were waited for; matrix products, arithmetic and copies ran while one was open for 2% of the time, Pallas kernels for 0%

profile of v1, /device:TPU:2, one launch (start us, length us, event | category | flops | bytes accessed | tf_op | source)
XLA Modules:
  0.0 506.8 jit_solution(11954460398220408562)
XLA Ops:
  11.8 2.9 scatter_custom_fusion
  15.4 9.4 %all-to-all-start = ((s32[32,1,9]{2,1,0:T(1,128)}), s32[32,1,9]{2,1,0:T(1,128)S(1)}, u32[]{:S(2)}, u32[]{:S(2)}) async-start(s32[32,1,9]{2,1,0:T(1,128)} %bitcast.28), calls=%async_computation | async-start | bytes 32768 | tf_op jit(solution)/shard_map/all_to_all | solution.py:74
  27.8 2.3 gather_fusion.2
  31.3 1.4 gather_fusion
  33.8 6.6 %all-to-all-start.1 = ((bf16[32,9,128]{2,1,0:T(8,128)(2,1)}), bf16[32,9,128]{2,1,0:T(8,128)(2,1)S(1)}, u32[]{:S(2)}, u32[]{:S(2)}) async-start(bf16[32,9,128]{2,1,0:T(8,128)(2,1)} %select_select_fusion), calls=%async_computation.1 | async-start | bytes 262144 | tf_op jit(solution)/shard_map/all_to_all | solution.py:78
  40.5 6.5 %all-to-all-done.1 = bf16[32,9,128]{2,1,0:T(8,128)(2,1)S(1)} async-done(((bf16[32,9,128]{2,1,0:T(8,128)(2,1)}), bf16[32,9,128]{2,1,0:T(8,128)(2,1)S(1)}, u32[]{:S(2)}, u32[]{:S(2)}) %all-to-all-start.1) | async-done | bytes 73760 | tf_op jit(solution)/shard_map/all_to_all | solution.py:78
  47.1 1.4 gather_fusion.1
  49.4 165.9 %while.12 = (s32[]{:T(128)}, f32[8]{0:T(128)}, f32[8,39,128]{2,1,0:T(8,128)}, bf16[8,39,128]{2,1,0:T(8,128)(2,1)}, bf16[100,1521]{1,0:T(8,128)(2,1)S(1)}, /*inde...) while((s32[]{:T(128)}, f32[8]{0:T(128)}, ...), condition=%wide.region_17.18_spmd, body=%wide.region_4.17_spmd.sunk | while | flops 484535232 | bytes 39531044 | solution.py:96
  51.2 1.6 fusion.65
  53.3 1.7 fusion.66
  57.7 1.8 convolution_bitcast_fusion.6
  59.5 1.6 reshape.545
  62.3 1.8 convolution_bitcast_fusion.7
  64.1 1.6 reshape.546
  71.9 1.6 fusion.65
  74.1 1.7 fusion.66
  78.4 1.8 convolution_bitcast_fusion.6
  80.3 1.6 reshape.545
  83.0 1.8 convolution_bitcast_fusion.7
  84.9 1.6 reshape.546
  92.6 1.6 fusion.65
  94.8 1.7 fusion.66
  99.2 1.8 convolution_bitcast_fusion.6
  101.0 1.6 reshape.545
  103.7 1.8 convolution_bitcast_fusion.7
  105.6 1.6 reshape.546
  113.4 1.6 fusion.65
  115.5 1.7 fusion.66
  119.9 1.8 convolution_bitcast_fusion.6
  121.7 1.6 reshape.545
  124.5 1.8 convolution_bitcast_fusion.7
  126.3 1.6 reshape.546
  134.1 1.6 fusion.65
  136.3 1.7 fusion.66
  140.6 1.8 convolution_bitcast_fusion.6
  142.5 1.6 reshape.545
  145.2 1.8 convolution_bitcast_fusion.7
  147.1 1.6 reshape.546
  154.9 1.6 fusion.65
  157.0 1.7 fusion.66
  161.4 1.8 convolution_bitcast_fusion.6
  163.2 1.6 reshape.545
  166.0 1.8 convolution_bitcast_fusion.7
  167.8 1.6 reshape.546
  175.6 1.6 fusion.65
  177.8 1.7 fusion.66
  182.1 1.8 convolution_bitcast_fusion.6
  184.0 1.6 reshape.545
  186.7 1.8 convolution_bitcast_fusion.7
  188.6 1.6 reshape.546
  196.4 1.6 fusion.65
  198.5 1.7 fusion.66
  202.9 1.8 convolution_bitcast_fusion.6
  204.7 1.6 reshape.545
  207.5 1.8 convolution_bitcast_fusion.7
  209.3 1.6 reshape.546
  216.3 2.8 scatter_custom_fusion.1
  219.2 2.0 scatter_custom_fusion.2
  221.3 11.4 %all_to_all.19 = bf16[32,9,128]{2,1,0:T(8,128)(2,1)S(1)} all-to-all(bf16[32,9,128]{2,1,0:T(8,128)(2,1)S(1)} %convert_element_type.112), channel_id=1, replica_groups=mesh['group'=16,'shard'=32] {'shard'}, dimensions={0} | all-to-all | bytes 147456 | tf_op jit(solution)/shard_map/all_to_all | solution.py:102
  232.7 2.5 scatter_custom_fusion.3
  236.4 118.2 %all-reduce.6.cloned.1.call-done = f32[2048,128]{1,0:T(8,128)} async-done(((f32[2048,128]{1,0:T(8,128)}), f32[2048,128]{1,0:T(8,128)}) %all-reduce.6.cloned.1.call-update) | async-done | bytes 1048592 | tf_op jit(solution)/shard_map/psum | solution.py:114
  354.6 75.1 %all-reduce.9 = bf16[2048,128]{1,0:T(8,128)(2,1)} all-reduce(f32[2048,128]{1,0:T(8,128)} %all-reduce.6.cloned.1.call-done), channel_id=1, replica_groups=mesh['group'=16,'shard'=32] {'group'}, use_global_device_ids=true, to_apply=%region_20.21 | all-reduce | flops 262144 | bytes 1572864 | tf_op jit(solution)/shard_map/psum | solution.py:114
  429.7 68.1 %all-reduce.8.cloned.1.call-done = bf16[4096,128]{1,0:T(8,128)(2,1)} async-done(((bf16[4096,128]{1,0:T(8,128)(2,1)}), bf16[4096,128]{1,0:T(8,128)(2,1)}) %all-reduce.8.cloned.1.call-update) | async-done | bytes 1048592 | tf_op jit(solution)/shard_map/psum | solution.py:110
  497.7 2.3 copy.48
  (281 shorter events, 82.3 us)
Async XLA Ops:
  7.2 24.2 %copy-start = (bf16[4096,128]{1,0:T(8,128)(2,1)S(1)}, bf16[4096,128]{1,0:T(8,128)(2,1)}, u32[]{:S(2)}) copy-start(bf16[4096,128]{1,0:T(8,128)(2,1)} %param.19) | copy-start | bytes 3145732
  8.0 23.3 %copy-start.6 = (pred[312]{0:T(512)(128)(4,1)}, pred[312]{0:T(512)(128)(4,1)S(1)}, u32[]{:S(2)}) copy-start(pred[312]{0:T(512)(128)(4,1)S(1)} %eq.48) | copy-start | bytes 940
  11.8 36.7 %copy-start.8 = (s32[312]{0:T(512)}, s32[312]{0:T(512)S(1)}, u32[]{:S(2)}) copy-start(s32[312]{0:T(512)S(1)} %fusion.26) | copy-start | bytes 3748
  15.4 15.6 %all-to-all-start = ((s32[32,1,9]{2,1,0:T(1,128)}), s32[32,1,9]{2,1,0:T(1,128)S(1)}, u32[]{:S(2)}, u32[]{:S(2)}) async-start(s32[32,1,9]{2,1,0:T(1,128)} %bitcast.28), calls=%async_computation | async-start | bytes 32768 | tf_op jit(solution)/shard_map/all_to_all | solution.py:74
  27.8 21.6 %copy-start.3 = (bf16[100,1521]{1,0:T(8,128)(2,1)S(1)}, bf16[100,1521]{1,0:T(8,128)(2,1)}, u32[]{:S(2)}) copy-start(bf16[100,1521]{1,0:T(8,128)(2,1)} %param.20) | copy-start | bytes 912604
  27.8 21.6 %copy-start.5 = (f32[3,100]{1,0:T(4,128)S(1)}, f32[3,100]{1,0:T(4,128)}, u32[]{:S(2)}) copy-start(f32[3,100]{1,0:T(4,128)} %param.23) | copy-start | bytes 3604
  31.3 9.2 %copy-start.9 = (s32[288]{0:T(512)}, s32[288]{0:T(512)S(1)}, u32[]{:S(2)}) copy-start(s32[288]{0:T(512)S(1)} %reshape.473) | copy-start | bytes 3460
  33.8 13.2 %all-to-all-start.1 = ((bf16[32,9,128]{2,1,0:T(8,128)(2,1)}), bf16[32,9,128]{2,1,0:T(8,128)(2,1)S(1)}, u32[]{:S(2)}, u32[]{:S(2)}) async-start(bf16[32,9,128]{2,1,0:T(8,128)(2,1)} %select_select_fusion), calls=%async_computation.1 | async-start | bytes 262144 | tf_op jit(solution)/shard_map/all_to_all | solution.py:78
  40.5 314.1 %all-reduce.6.cloned.1.call-start = ((), (), s32[]{:S(2)}) async-start(), calls=%async_computation.3 | async-start | bytes 2097152 | tf_op jit(solution)/shard_map/psum | solution.py:114
  53.3 4.4 copy-start.2
  61.1 1.1 copy-start.1
  66.3 0.7 copy-start.4
  66.3 3.2 copy-start.10
  69.7 0.5 copy-start.11
  74.0 4.4 copy-start.2
  81.9 1.1 copy-start.1
  87.1 0.7 copy-start.4
  87.1 3.2 copy-start.10
  90.4 0.5 copy-start.11
  94.8 4.4 copy-start.2
  102.6 1.1 copy-start.1
  107.8 0.7 copy-start.4
  107.8 3.2 copy-start.10
  111.1 0.5 copy-start.11
  115.5 4.4 copy-start.2
  123.3 1.1 copy-start.1
  128.5 0.7 copy-start.4
  128.6 3.2 copy-start.10
  131.9 0.5 copy-start.11
  136.3 4.4 copy-start.2
  144.1 1.1 copy-start.1
  149.3 0.7 copy-start.4
  149.3 3.2 copy-start.10
  152.6 0.5 copy-start.11
  157.0 4.4 copy-start.2
  164.8 1.1 copy-start.1
  170.0 0.7 copy-start.4
  170.0 3.2 copy-start.10
  173.4 0.5 copy-start.11
  177.8 4.4 copy-start.2
  185.6 1.1 copy-start.1
  190.8 0.7 copy-start.4
  190.8 3.2 copy-start.10
  194.1 0.5 copy-start.11
  198.5 4.4 copy-start.2
  206.3 1.1 copy-start.1
  211.5 0.7 copy-start.4
  211.5 3.2 copy-start.10
  214.9 0.5 copy-start.11
  215.4 3.8 copy-start.7
  219.2 278.6 %all-reduce.8.cloned.1.call-start = ((), (), s32[]{:S(2)}) async-start(), calls=%async_computation.4 | async-start | bytes 2097152 | tf_op jit(solution)/shard_map/psum | solution.py:110
Sparse Core Ops, SparseCore 0:
  219.3 135.2 all-reduce.5
  356.9 140.7 all-reduce.7
